TPU v7x, 512 devices: a whole 4x4x16 slice. The times are simulated.
512 devices in a mesh: grp: 16 (over y, x), sp: 32 (over z, core).
Axes of the slice: x: 4, y: 4, z: 16, core: 2. Of those that a mesh axis runs over, the one named last changes fastest.
Arguments:
- coarse: bfloat16 [1024, 48, 1024], P(('grp', 'sp')), parts along dimension 0, may hold values from -30 to 30
- conv_weight: bfloat16 [1024, 3, 3, 1024], P('sp'), may hold values from -0.104166667 to 0.104166667
- conv_bias: float32 [1024], P('sp'), may hold values from -5 to 5
- norm_gain: float32 [1024], P('sp'), may hold values from 0.5 to 1.5
- norm_shift: float32 [1024], P('sp'), may hold values from -3 to 3
- up_weight: bfloat16 [512, 2, 2, 1024], P('sp'), may hold values from -0.1875 to 0.1875
- up_bias: bfloat16 [512], P('sp'), may hold values from -3 to 3
Outputs:
- fine: bfloat16 [2048, 96, 512], P(('grp', 'sp')), parts along dimension 0
There are 16 independent parts, one for each index of `grp`. A program takes and returns all parts, laid end to end along the dimension named above; an argument that names none is the same for every part. Nothing has to cross between parts.
All inputs are finite; a program needn't handle non-finite values.
Results may differ from a plain program's by a relative error of at most 0.0042.
Values may be sent and summed in bfloat16 or wider, within the bound.
No kernel may reach another device: no remote copies, remote signals or barrier semaphores. Data moves between devices by JAX's collectives and lax.ppermute only.
A program may use at most 64 MiB of HBM per device.

v0:
```python
import jax
import jax.numpy as jnp
from jax import lax
from jax.sharding import PartitionSpec as P

GSIZE = 32


def conv_rows(weights_cat, width_cols, channels, outputs, tile_rows):
    how_many = tile_rows.shape[0]
    padded = jnp.pad(tile_rows, ((0, 0), (1, 1), (0, 0)))
    partial_sum = jnp.zeros((how_many * width_cols, 3 * outputs), jnp.float32)
    for offset in range(3):
        window = padded[:, offset : offset + width_cols, :].reshape(how_many * width_cols, channels)
        partial_sum = partial_sum + jnp.dot(
            window, weights_cat[offset], preferred_element_type=jnp.float32
        )
    partial_sum = partial_sum.reshape(how_many, width_cols, 3, outputs)
    contrib = jnp.zeros((how_many + 2, width_cols, outputs), jnp.float32)
    for kernel_row in range(3):
        contrib = contrib.at[2 - kernel_row : 2 - kernel_row + how_many].add(
            partial_sum[:, :, kernel_row]
        )
    return contrib


def normalize(convolved, height, width_cols, outputs, norm_gain, norm_shift):
    grouped = convolved.reshape(height, width_cols, outputs // GSIZE, GSIZE)
    centre = jnp.mean(grouped, axis=(0, 1, 3), keepdims=True)
    spread = jnp.mean(jnp.square(grouped - centre), axis=(0, 1, 3), keepdims=True)
    normed = ((grouped - centre) * lax.rsqrt(spread + 1e-05)).reshape(height, width_cols, outputs)
    return jax.nn.silu(normed * norm_gain + norm_shift).astype(jnp.bfloat16)


def full_conv(coarse, conv_weight, conv_bias, norm_gain, norm_shift):
    tile_count = lax.axis_size("sp")
    local_rows, width_cols, channels = coarse.shape
    height = local_rows * tile_count
    outputs = conv_weight.shape[0]
    weights_cat = jnp.transpose(conv_weight, (2, 3, 1, 0)).reshape(3, channels, 3 * outputs)
    summed = conv_rows(
        weights_cat, width_cols, channels, outputs, lax.all_gather(coarse, "sp", axis=0, tiled=True)
    )
    convolved = summed[1 : height + 1] + conv_bias
    return normalize(convolved, height, width_cols, outputs, norm_gain, norm_shift)


def body(coarse, conv_weight, conv_bias, norm_gain, norm_shift, up_weight, up_bias):
    activated = full_conv(coarse, conv_weight, conv_bias, norm_gain, norm_shift)
    height, width_cols, channels = (activated.shape[0], activated.shape[1], conv_weight.shape[3])
    slice_out = up_weight.shape[0]
    flat_weight = jnp.transpose(up_weight, (3, 1, 2, 0)).reshape(channels, 4 * slice_out)
    features = lax.all_gather(activated, "sp", axis=2, tiled=True)
    chosen_width = features.shape[2]
    flat_features = features.reshape(height * width_cols, chosen_width)
    decoded = jnp.dot(flat_features, flat_weight, preferred_element_type=jnp.float32)
    decoded = (decoded.reshape(height, width_cols, 2, 2, slice_out) + up_bias).astype(jnp.bfloat16)
    decoded = jnp.transpose(decoded, (0, 2, 1, 3, 4)).reshape(2 * height, 2 * width_cols, slice_out)
    return lax.all_to_all(decoded, "sp", split_axis=0, concat_axis=2, tiled=True)


def solution(mesh):
    return jax.shard_map(
        body,
        mesh=mesh,
        in_specs=(
            P(("grp", "sp"), None, None),
            P("sp", None, None, None),
            P("sp"),
            P("sp"),
            P("sp"),
            P("sp", None, None, None),
            P("sp"),
        ),
        out_specs=P(("grp", "sp"), None, None),
        check_vma=False,
    )
```

profile of v0, /device:TPU:1, one launch (start us, length us, event | category | flops | bytes accessed | tf_op | source)
XLA Modules:
  0.0 294.0 jit_solution(15745474738051141578)
XLA Ops:
  6.5 0.0 all-gather.3.cloned.1.call-start
  6.5 0.7 all-gather.3.cloned.1.call-update
  7.3 0.0 all-gather.5.cloned.1.call-start
  7.3 1.2 fusion.14
  8.5 83.6 %all-gather.3.cloned.1.call-done = bf16[64,48,1024]{2,1,0:T(8,128)(2,1)} async-done(((bf16[2,48,1024]{2,1,0:T(8,128)(2,1)}), bf16[64,48,1024]{2,1,0:T(8,128)(2,1)}) %all-gather.3.cloned.1.call-update) | async-done | bytes 6291472 | tf_op jit(solution)/shard_map/all_gather | solution.py:42
  92.1 10.7 %pad_slice_fusion = (bf16[64,48,1024]{2,1,0:T(8,128)(2,1)S(1)}, bf16[64,48,1024]{2,1,0:T(8,128)(2,1)S(1)}) fusion(bf16[64,48,1024]{2,1,0:T(8,128)(2,1)} %all-gather.3.cloned.1.call-done), kind=kLoop, calls=%fused_computation.2 | loop fusion | bytes 18874368 | tf_op jit(solution)/shard_map/slice | solution.py:14
  102.9 0.0 copy-start
  102.9 2.0 fusion.15
  104.9 0.7 copy-done
  105.7 2.0 convolution_add_fusion.1
  107.7 3.1 %convolution_add_fusion = f32[3072,96]{0,1:T(8,128)} fusion(f32[3072,96]{0,1:T(8,128)S(1)} %convolution_add_fusion.1, bf16[3072,1024]{1,0:T(8,128)(2,1)S(1)} %bitcast.56, bf16[1024,96]{0,1:T(8,128)(2,1)S(1)} %bitcast.62), kind=kOutput, calls=%fused_computation.4 | convolution fusion | flops 604274688 | bytes 8847360 | tf_op jit(solution)/shard_map/dot_general | solution.py:15
  110.8 2.6 reshape.152
  113.4 0.2 fusion.13
  113.7 0.6 copy.44
  114.3 0.1 scatter-add.10
  114.4 0.0 copy-start.2
  114.4 1.0 fusion.9
  115.4 0.0 copy-start.3
  115.4 0.0 copy-start.4
  115.4 0.0 copy-start.5
  115.4 0.0 copy-start.1
  115.4 1.0 fusion.7
  116.4 0.0 copy-done.2
  116.4 1.0 fusion.10
  118.0 0.9 multiply_reduce_fusion
  119.7 0.0 copy-done.3
  119.7 0.0 copy-done.4
  119.7 1.3 multiply_convert_fusion
  120.9 0.0 all-gather.5.cloned.1.call-update
  121.0 0.0 copy-done.5
  121.0 104.1 %all-gather.5.cloned.1.call-done = bf16[64,48,1024]{1,2,0:T(8,128)(2,1)} async-done(((bf16[64,48,32]{1,2,0:T(8,128)(2,1)}), bf16[64,48,1024]{1,2,0:T(8,128)(2,1)}) %all-gather.5.cloned.1.call-update) | async-done | bytes 6291472 | tf_op jit(solution)/shard_map/all_gather | solution.py:53
  225.0 0.0 copy-done.1
  225.1 9.7 %fusion.4 = bf16[64,2,48,2,16]{2,4,3,1,0:T(8,128)(2,1)} fusion(bf16[64,48,1024]{1,2,0:T(8,128)(2,1)} %all-gather.5.cloned.1.call-done, f32[16]{0:T(128)S(1)} %convert_element_type.16, bf16[16,2,2,1024]{3,2,1,0:T(2,128)(2,1)S(1)} %copy-done.1), kind=kOutput, calls=%fused_computation.7 | convolution fusion | flops 403046400 | bytes 6815808 | tf_op jit(solution)/shard_map/dot_general | solution.py:56
  234.8 6.1 %copy.23 = bf16[64,2,48,2,16]{4,3,2,1,0:T(2,128)(2,1)S(1)} copy(bf16[64,2,48,2,16]{2,4,3,1,0:T(8,128)(2,1)} %fusion.4) | data formatting | bytes 786432 | tf_op jit(solution)/shard_map/convert_element_type | solution.py:57
  240.9 2.7 copy.24
  243.5 42.6 %all_to_all.18 = bf16[128,96,16]{1,2,0:T(8,128)(2,1)S(1)} all-to-all(bf16[128,96,16]{1,2,0:T(8,128)(2,1)} %copy.24), channel_id=1, replica_groups=mesh['grp'=16,'sp'=32] {'sp'}, dimensions={0} | all-to-all | bytes 786432 | tf_op jit(solution)/shard_map/all_to_all | solution.py:59
  286.2 1.0 copy.26
  (2 shorter events, 0.0 us)
Async XLA Ops:
  6.5 85.6 %all-gather.3.cloned.1.call-start = ((), (), s32[]{:S(2)}) async-start(), calls=%async_computation.1 | async-start | bytes 6488064 | tf_op jit(solution)/shard_map/all_gather | solution.py:42
  7.3 217.8 %all-gather.5.cloned.1.call-start = ((), (), s32[]{:S(2)}) async-start(), calls=%async_computation.2 | async-start | bytes 17301504 | tf_op jit(solution)/shard_map/all_gather | solution.py:53
  102.9 2.8 copy-start
  114.4 2.0 copy-start.2
  115.4 4.3 %copy-start.3 = (f32[32]{0:T(128)S(1)}, f32[32]{0:T(128)}, u32[]{:S(2)}) copy-start(f32[32]{0:T(128)} %param.17) | copy-start | bytes 388
  115.4 4.3 %copy-start.4 = (f32[32]{0:T(128)S(1)}, f32[32]{0:T(128)}, u32[]{:S(2)}) copy-start(f32[32]{0:T(128)} %param.16) | copy-start | bytes 388
  115.4 5.6 %copy-start.5 = (bf16[16]{0:T(256)(128)(2,1)S(1)}, bf16[16]{0:T(256)(128)(2,1)}, u32[]{:S(2)}) copy-start(bf16[16]{0:T(256)(128)(2,1)} %param.19) | copy-start | bytes 100
  115.4 109.6 %copy-start.1 = (bf16[16,2,2,1024]{3,2,1,0:T(2,128)(2,1)S(1)}, bf16[16,2,2,1024]{3,2,1,0:T(2,128)(2,1)}, u32[]{:S(2)}) copy-start(bf16[16,2,2,1024]{3,2,1,0:T(2,128)(2,1)} %param.18) | copy-start | bytes 393220
Sparse Core Ops, SparseCore 0:
  9.5 82.6 all-gather.2
  121.1 103.9 all-gather.4
where the time goes:
time: 294 us
  waiting for transfers between devices  188 us (64%)
  blocking collectives  42.6 us (14%)
  local copies, waits for them, and re-layouts  26 us (9%)
  matrix products  16.9 us (6%)
  between operations  14.9 us (5%)
  other arithmetic  5.12 us (2%)
    all_gather x1, waiting for transfers between devices, body(): features = lax.all_gather(activated, 'sp', axis=2, tiled=True)  104 us
    all_gather x1, waiting for transfers between devices, full_conv(): lax.all_gather(coarse, 'sp', axis=0, tiled=True)  83.6 us
    all_to_all x1, blocking collectives, body(): lax.all_to_all(decoded, 'sp', split_axis=0, concat_axis=2, tiled=True)  42.6 us
    slice x1, local copies, waits for them, and re-layouts, conv_rows(): padded[:, offset:offset + width_cols, :]  10.7 us
    dot_general x1, matrix products, body(): jnp.dot(flat_features, flat_weight, preferred_element_type=jnp.float32)  9.72 us
    dot_general x3, matrix products, conv_rows(): jnp.dot(window, weights_cat[offset], preferred_element_type=jnp.float32)  7.18 us
    convert_element_type x1, local copies, waits for them, and re-layouts, body(): (decoded.reshape(height, width_cols, 2, 2, slice_out) + up_bias).astype(j...  6.09 us
  transfers between devices with their start and end apart: 2, of which 2 were waited for; matrix products, arithmetic and copies ran while one was open for 0% of the time, Pallas kernels for 0%

commit v1 on v0

--- a/solution.py
+++ b/solution.py
@@ -50,7 +50,9 @@
     height, width_cols, channels = (activated.shape[0], activated.shape[1], conv_weight.shape[3])
     slice_out = up_weight.shape[0]
     flat_weight = jnp.transpose(up_weight, (3, 1, 2, 0)).reshape(channels, 4 * slice_out)
-    features = lax.all_gather(activated, "sp", axis=2, tiled=True)
+    features = jnp.concatenate(
+        lax.all_to_all(jnp.stack([activated] * lax.axis_size("sp")), "sp", 0, 0), axis=2
+    )
     chosen_width = features.shape[2]
     flat_features = features.reshape(height * width_cols, chosen_width)
     decoded = jnp.dot(flat_features, flat_weight, preferred_element_type=jnp.float32)

time: 294 us -> 539 us (1.83)
  waiting for transfers between devices: 188 us -> 359 us
  local copies, waits for them, and re-layouts: 26 us -> 96.1 us
  starting transfers between devices: 0.04 us -> 8.58 us
  matrix products: 16.9 us -> 10.3 us
    all_to_all x0 -> x1, waiting for transfers between devices: none -> 275 us  [body(): lax.all_to_all(jnp.stack([activated] * lax.axis_size('sp')), 'sp', 0, 0)]
    all_gather x1 -> x0, waiting for transfers between devices: 104 us -> none  [body(): features = lax.all_gather(activated, 'sp', axis=2, tiled=True)]
    unnamed x13 -> x17, local copies, waits for them, and re-layouts: 1.37 us -> 57.3 us
    reshape x0 -> x2, local copies, waits for them, and re-layouts: none -> 8.73 us  [body(): jnp.concatenate(lax.all_to_all(jnp.stack([activated] * lax.axis_size('sp'...]
    all_to_all x0 -> x1, starting transfers between devices: none -> 8.58 us  [body(): lax.all_to_all(jnp.stack([activated] * lax.axis_size('sp')), 'sp', 0, 0)]
    dot_general x1, matrix products: 9.72 us -> 3.14 us  [body(): jnp.dot(flat_features, flat_weight, preferred_element_type=jnp.float32)]
where the time goes in v1:
time: 539 us; the launch traced here: 537 us
  waiting for transfers between devices  359 us (67%)
  local copies, waits for them, and re-layouts  96.1 us (18%)
  blocking collectives  42.3 us (8%)
  between operations  14.9 us (3%)
  matrix products  10.3 us (2%)
  starting transfers between devices  8.58 us (2%)
    all_to_all x1, waiting for transfers between devices, body(): lax.all_to_all(jnp.stack([activated] * lax.axis_size('sp')), 'sp', 0, 0)  275 us
    all_gather x1, waiting for transfers between devices, full_conv(): lax.all_gather(coarse, 'sp', axis=0, tiled=True)  83.7 us
    unnamed x17, local copies, waits for them, and re-layouts  57.3 us
    all_to_all x1, blocking collectives, body(): lax.all_to_all(decoded, 'sp', split_axis=0, concat_axis=2, tiled=True)  42.3 us
  transfers between devices with their start and end apart: 2, of which 2 were waited for; matrix products, arithmetic and copies ran while one was open for 0% of the time, Pallas kernels for 0%

profile of v1, /device:TPU:1, one launch (start us, length us, event | category | flops | bytes accessed | tf_op | source)
XLA Modules:
  0.0 536.7 jit_solution(13708723689854922937)
XLA Ops:
  6.5 0.0 all-gather.2.cloned.1.call-start
  6.5 0.7 all-gather.2.cloned.1.call-update
  7.3 1.2 fusion.7
  8.4 83.7 %all-gather.2.cloned.1.call-done = bf16[64,48,1024]{2,1,0:T(8,128)(2,1)} async-done(((bf16[2,48,1024]{2,1,0:T(8,128)(2,1)}), bf16[64,48,1024]{2,1,0:T(8,128)(2,1)}) %all-gather.2.cloned.1.call-update) | async-done | bytes 6291472 | tf_op jit(solution)/shard_map/all_gather | solution.py:42
  92.1 10.7 %pad_slice_fusion = (bf16[64,48,1024]{2,1,0:T(8,128)(2,1)S(1)}, bf16[64,48,1024]{2,1,0:T(8,128)(2,1)S(1)}) fusion(bf16[64,48,1024]{2,1,0:T(8,128)(2,1)} %all-gather.2.cloned.1.call-done), kind=kLoop, calls=%fused_computation | loop fusion | bytes 18874368 | tf_op jit(solution)/shard_map/slice | solution.py:14
  102.9 0.0 copy-start
  102.9 2.0 fusion.8
  104.9 0.7 copy-done
  105.7 2.0 convolution_add_fusion.1
  107.7 3.1 convolution_add_fusion
  110.8 2.4 reshape.157
  113.3 0.0 copy-start.1
  113.3 0.0 copy-start.3
  113.3 0.1 slice_bitcast_fusion.2
  113.4 1.5 copy-done.1
  114.9 0.0 copy-start.4
  114.9 0.0 copy-start.5
  114.9 1.2 fusion.3
  116.1 0.1 scatter-add.10
  116.3 5.2 scatter-add.11
  121.5 1.5 fusion.2
  123.0 0.0 copy-done.3
  123.0 1.0 fusion.4
  124.6 1.0 multiply_reduce_fusion
  126.3 0.0 copy-done.4
  126.4 0.0 copy-done.5
  126.4 0.6 multiply_convert_fusion
  127.0 0.6 copy.16
  127.6 7.4 %broadcast_bitcast_fusion = bf16[32,48,32,64]{3,2,1,0:T(8,128)(2,1)} fusion(bf16[64,48,32]{0,2,1:T(8,128)(2,1)S(1)} %copy.16), kind=kLoop, calls=%fused_computation.20 | loop fusion | bytes 6488064
  134.9 24.2 %reshape.165 = bf16[32,2,49152]{2,1,0:T(2,128)(2,1)} reshape(bf16[32,48,32,64]{3,2,1,0:T(8,128)(2,1)} %broadcast_bitcast_fusion) | data formatting | bytes 12582912
  159.1 0.0 copy-start.6
  159.1 8.6 %all-to-all-start = ((bf16[32,2,49152]{2,1,0:T(2,128)(2,1)}), bf16[32,2,49152]{2,1,0:T(2,128)(2,1)}, u32[]{:S(2)}, u32[]{:S(2)}) async-start(bf16[32,2,49152]{2,1,0:T(2,128)(2,1)} %reshape.165), calls=%async_computation | async-start | bytes 12582912 | tf_op jit(solution)/shard_map/all_to_all | solution.py:54
  167.7 0.0 copy-done.6
  167.7 274.7 %all-to-all-done = bf16[32,2,49152]{2,1,0:T(2,128)(2,1)} async-done(((bf16[32,2,49152]{2,1,0:T(2,128)(2,1)}), bf16[32,2,49152]{2,1,0:T(2,128)(2,1)}, u32[]{:S(2)}, u32[]{:S(2)}) %all-to-all-start) | async-done | bytes 6291488 | tf_op jit(solution)/shard_map/all_to_all | solution.py:54
  442.4 23.4 %reshape.166 = bf16[32,48,32,64]{3,2,1,0:T(8,128)(2,1)} reshape(bf16[32,2,49152]{2,1,0:T(2,128)(2,1)} %all-to-all-done) | data formatting | bytes 12582912
  465.9 7.2 %bitcast_bitcast_fusion = bf16[64,48,32,32]{0,3,1,2:T(8,128)(2,1)S(1)} fusion(bf16[32,48,32,64]{3,2,1,0:T(8,128)(2,1)} %reshape.166), kind=kLoop, calls=%fused_computation.19 | loop fusion | bytes 12582912 | tf_op jit(solution)/shard_map/reshape | solution.py:53
  473.1 0.0 copy-start.2
  473.1 1.5 copy.17
  474.6 0.0 copy-done.2
  474.7 3.1 fusion
  477.8 6.1 %copy.20 = bf16[64,2,48,2,16]{4,3,2,1,0:T(2,128)(2,1)S(1)} copy(bf16[64,2,48,2,16]{0,4,3,1,2:T(8,128)(2,1)} %fusion) | data formatting | bytes 786432 | tf_op jit(solution)/shard_map/convert_element_type | solution.py:59
  483.9 2.7 copy.21
  486.5 42.3 %all_to_all.23 = bf16[128,96,16]{1,2,0:T(8,128)(2,1)S(1)} all-to-all(bf16[128,96,16]{1,2,0:T(8,128)(2,1)} %copy.21), channel_id=1, replica_groups=mesh['grp'=16,'sp'=32] {'sp'}, dimensions={0} | all-to-all | bytes 786432 | tf_op jit(solution)/shard_map/all_to_all | solution.py:61
  528.9 1.0 copy.23
  (2 shorter events, 0.0 us)
Async XLA Ops:
  6.5 85.6 %all-gather.2.cloned.1.call-start = ((), (), s32[]{:S(2)}) async-start(), calls=%async_computation.2 | async-start | bytes 6488064 | tf_op jit(solution)/shard_map/all_gather | solution.py:42
  102.9 2.8 copy-start
  113.3 1.6 copy-start.1
  113.3 9.7 %copy-start.3 = (f32[32]{0:T(128)S(1)}, f32[32]{0:T(128)}, u32[]{:S(2)}) copy-start(f32[32]{0:T(128)} %param.15) | copy-start | bytes 388
  114.9 11.4 %copy-start.4 = (f32[32]{0:T(128)S(1)}, f32[32]{0:T(128)}, u32[]{:S(2)}) copy-start(f32[32]{0:T(128)} %param.17) | copy-start | bytes 388
  114.9 11.4 %copy-start.5 = (f32[32]{0:T(128)S(1)}, f32[32]{0:T(128)}, u32[]{:S(2)}) copy-start(f32[32]{0:T(128)} %param.16) | copy-start | bytes 388
  159.1 8.6 %copy-start.6 = (bf16[16]{0:T(256)(128)(2,1)S(1)}, bf16[16]{0:T(256)(128)(2,1)}, u32[]{:S(2)}) copy-start(bf16[16]{0:T(256)(128)(2,1)} %param.19) | copy-start | bytes 100
  159.1 283.3 %all-to-all-start = ((bf16[32,2,49152]{2,1,0:T(2,128)(2,1)}), bf16[32,2,49152]{2,1,0:T(2,128)(2,1)}, u32[]{:S(2)}, u32[]{:S(2)}) async-start(bf16[32,2,49152]{2,1,0:T(2,128)(2,1)} %reshape.165), calls=%async_computation | async-start | bytes 12582912 | tf_op jit(solution)/shard_map/all_to_all | solution.py:54
  473.1 1.5 copy-start.2
Sparse Core Ops, SparseCore 0:
  9.5 82.6 all-gather.1
